TPU v7x, 256 devices: a whole 4x4x8 slice. The times are simulated.
256 devices in a mesh: row: 16 (over x_lo, y, core), col: 16 (over z, x_hi).
Axes of the slice: x: 4 (x_hi: 2, x_lo: 2; x = x_hi * 2 + x_lo), y: 4, z: 8, core: 2. Of those that a mesh axis runs over, the one named last changes fastest.
Arguments:
- adj_values: bfloat16 [2, 16, 16, 20, 128, 128], P(None, 'row', 'col'), may hold values from -6 to 6
- block_rows: int32 [2, 16, 16, 20], P(None, 'row', 'col'), may hold values from 0 to 47, as said below
- block_cols: int32 [2, 16, 16, 20], P(None, 'row', 'col'), may hold values from 0 to 15, as said below
- block_counts: int32 [2, 16, 16], P(None, 'row', 'col'), may hold values from 5 to 20, as said below
- block_scales: bfloat16 [2, 16, 16, 20], P(None, 'row', 'col'), may hold values from 0.0049743652 to 0.049804688
- panel_features: bfloat16 [2, 256, 32768], P(None, 'col', 'row'), may hold values from -6 to 6
- weight: bfloat16 [256, 256], replicated, may hold values from -0.375 to 0.375
- out_bias: float32 [256], replicated, may hold values from -3 to 3
Outputs:
- layer_out: bfloat16 [98304, 256], P(('row', 'col'))
Inputs may be any that keep to these rules, and one draw needn't show every extreme that they name: `block_rows`: block rows are local to the 48 block rows of a row index. The slots of one device in one panel name distinct (block row, block column) pairs. `block_cols`: block columns index the 16 block columns of a col index's part of the panel. `block_counts`: in every panel, all devices of at least one row index hold exactly 20 live blocks.
All inputs are finite; a program needn't handle non-finite values.
Results may differ from a plain program's by a relative error of at most 0.0044.
Values may be sent and summed in bfloat16 or wider, within the bound.
No kernel may reach another device: no remote copies, remote signals or barrier semaphores. Data moves between devices by JAX's collectives and lax.ppermute only.
A program may use at most 64 MiB of HBM per device.

v0:
```python
import jax
import jax.numpy as jnp
from jax import lax
from jax.experimental import pallas as pl
from jax.experimental.pallas import tpu as pltpu
from jax.sharding import Mesh
from jax.sharding import PartitionSpec as P

ROWS = 48
BS = 128
MAXB = 20
STEPS = 2
NZ = 8
HALF = 128
GROUP = 4
ROW = ("xl", "y", "core")
COL = ("z", "xh")
SWAP = [(0, 1), (1, 0)]


def shift(n, by):
    return [(i, (i + by) % n) for i in range(n)]


def shift_and_cross(by):
    return [(z * 2 + h, (z + by) % NZ * 2 + 1 - h) for z in range(NZ) for h in range(2)]


def to_plane(k):
    pairs = []
    for xl in range(2):
        for y in range(4):
            for z in range(NZ):
                source_xl = xl if z // 4 == k else 1 - xl
                pairs.append(((xl * 4 + y) * NZ + z, (xl * 4 + z % 4) * NZ + source_xl * 4 + y))
    return pairs


def block_kernel(own, par, feats0, feats1, adj_own, adj_par, part, fwd, bwd, cross):
    core, xl = lax.axis_index("core"), lax.axis_index("xl")
    z, xh = lax.axis_index("z"), lax.axis_index("xh")
    flip = jnp.where(xl == z // 4, 0, 1)
    part[...] = jnp.zeros_like(part)

    def run(feats, adj, table):
        for t in range(STEPS):
            live = table[6 + t, 0].astype(jnp.int32)

            def group(g, carry):
                prods = []
                for u in range(GROUP):
                    slot = g * GROUP + u
                    at = pl.ds(pl.multiple_of(table[2 + t, slot].astype(jnp.int32) * BS, BS), BS)
                    x = jnp.concatenate([feats[p ^ flip, t, :, at] for p in range(8)], axis=0)
                    prods.append(
                        lax.dot_general(
                            adj[t * MAXB + slot], x, (((1,), (1,)), ((), ())), preferred_element_type=jnp.float32
                        )
                    )
                for u in range(GROUP):
                    slot = g * GROUP + u
                    row = table[t, slot].astype(jnp.int32)
                    stop = (row // 6 - z) & (NZ - 1)
                    place = stop * 6 + (((row // 3) & 1) ^ xh) * 3 + row % 3
                    scale = jnp.where(slot < live, table[4 + t, slot], 0.0)
                    part[place] = part[place] + prods[u] * scale
                return carry

            lax.fori_loop(0, (live + GROUP - 1) // GROUP, group, 0)

    @pl.when(core == xh)
    def _():
        run(feats0, adj_own, own)
        run(feats1, adj_par, par)

    @pl.when(core != xh)
    def _():
        run(feats1, adj_own, own)
        run(feats0, adj_par, par)

    for i, place in enumerate((24, 21)):
        fwd[i] = part[pl.ds(place, 3)].astype(fwd.dtype)
    for i, place in enumerate((27, 30)):
        bwd[i] = part[pl.ds(place, 3)].astype(bwd.dtype)
    cross[...] = part[pl.ds(3, 3)].astype(cross.dtype)


def block_products(own, par, feats0, feats1, adj_own, adj_par):
    smem = pl.BlockSpec(memory_space=pltpu.SMEM)
    vmem = pl.BlockSpec(memory_space=pltpu.VMEM)
    message = jax.ShapeDtypeStruct((2, 3, BS, HALF), jnp.bfloat16)
    return pl.pallas_call(
        block_kernel,
        out_shape=(
            jax.ShapeDtypeStruct((ROWS, BS, HALF), jnp.float32),
            message,
            message,
            jax.ShapeDtypeStruct((3, BS, HALF), jnp.bfloat16),
        ),
        in_specs=[smem, smem, vmem, vmem, vmem, vmem],
        out_specs=(vmem, vmem, vmem, vmem),
        cost_estimate=pl.CostEstimate(flops=80 * 2 * BS**3, bytes_accessed=9 << 20, transcendentals=0),
        name="block_products",
    )(own, par, feats0, feats1, adj_own, adj_par)


def body(adj_values, block_rows, block_cols, block_counts, block_scales, features, weight, out_bias):
    y = lax.axis_index("y")
    z, xh = (lax.axis_index(a) for a in COL)
    swapped = lax.ppermute(features, "xl", SWAP)
    adj = adj_values.reshape(STEPS * MAXB, BS, BS)
    adj_par = lax.ppermute(adj, "xh", SWAP)
    slots = (STEPS, MAXB)
    table = jnp.concatenate(
        [
            block_rows.reshape(slots).astype(jnp.float32),
            block_cols.reshape(slots).astype(jnp.float32),
            block_scales.reshape(slots).astype(jnp.float32),
            jnp.broadcast_to(block_counts.reshape(STEPS, 1), slots).astype(jnp.float32),
        ]
    )
    table_par = lax.ppermute(table, "xh", SWAP)

    low_plane = z < 4
    first = lax.ppermute(jnp.where(low_plane, features, swapped), ("xl", "y", "z"), to_plane(0))
    second = lax.ppermute(jnp.where(low_plane, swapped, features), ("xl", "y", "z"), to_plane(1))
    here = jnp.stack([first, second])
    below = lax.ppermute(here, "y", shift(4, 1))
    above = lax.ppermute(here, "y", shift(4, -1))
    far0 = lax.ppermute(below[:1], "y", shift(4, 1))
    far1 = lax.ppermute(above[1:], "y", shift(4, -1))
    feats0 = jnp.concatenate([here, below, above, far0, far1])
    feats1 = lax.ppermute(feats0, "core", SWAP)

    part, fwd, bwd, cross = block_products(table, table_par, feats0, feats1, adj, adj_par)
    part = part.reshape(NZ, 2, 3, BS, HALF)

    def low(v):
        return v.astype(jnp.bfloat16)

    def full(v):
        return v.astype(jnp.float32)

    ahead, back = shift(NZ, 1), shift(NZ, -1)
    got_f = full(lax.ppermute(fwd, "z", ahead))
    got_b = full(lax.ppermute(bwd, "z", back))
    crossed = full(lax.ppermute(cross, "xh", SWAP))
    fwd = low(got_f + jnp.stack([part[3, 0], part[2, 1]]))
    bwd = low(got_b + jnp.stack([part[5, 1], part[6, 0]]))
    got_f = full(lax.ppermute(fwd, "z", ahead))
    got_b = full(lax.ppermute(bwd, "z", back))
    fwd = low(got_f[0] + part[2, 0])
    fwd_cross = low(got_f[1] + part[1, 1])
    bwd = low(got_b + jnp.stack([part[6, 1], part[7, 0]]))
    got_f = full(lax.ppermute(fwd, "z", ahead))
    got_b = full(lax.ppermute(bwd, "z", back))
    crossed_f = full(lax.ppermute(fwd_cross, COL, shift_and_cross(1)))
    last_f = full(lax.ppermute(low(got_f + part[1, 0]), "z", ahead))
    crossed_b = full(lax.ppermute(low(got_b[0] + part[7, 1]), COL, shift_and_cross(-1)))
    mine = low(part[0, 0] + last_f + got_b[1])
    other = low(crossed + crossed_f + crossed_b)

    w = weight.reshape(2, 4, 2, 16, 256)
    w = jnp.concatenate([w, w], axis=1)
    w = lax.dynamic_slice_in_dim(w, y, 4, axis=1)
    w = jnp.stack([w[:, i] for i in (0, 3, 1, 2)])
    w_mine = jnp.where(xh == 0, w[:, :, 0], w[:, :, 1]).reshape(HALF, 256)
    w_other = jnp.where(xh == 0, w[:, :, 1], w[:, :, 0]).reshape(HALF, 256)
    before = jnp.dot(mine.reshape(-1, HALF), w_mine, preferred_element_type=jnp.float32)
    before = before + jnp.dot(other.reshape(-1, HALF), w_other, preferred_element_type=jnp.float32)
    return jax.nn.relu(before + out_bias).astype(jnp.bfloat16)


def solution(mesh):
    split = Mesh(mesh.devices.reshape(2, 4, 2, 8, 2), ROW + COL)
    in_specs = (
        P(None, ROW, COL, None, None, None),
        P(None, ROW, COL, None),
        P(None, ROW, COL, None),
        P(None, ROW, COL),
        P(None, ROW, COL, None),
        P(None, COL, ROW),
        P(),
        P(),
    )
    return jax.shard_map(body, mesh=split, in_specs=in_specs, out_specs=P(ROW + COL, None), check_vma=False)
```

profile of v0, /device:TPU:4, one launch (start us, length us, event | category | flops | bytes accessed | tf_op | source)
XLA Modules:
  0.0 99.9 jit_solution(602291757567615571)
XLA Ops:
  0.0 1.3 %collective-permute-start.1 = (bf16[2,16,2048]{2,1,0:T(8,128)(2,1)}, bf16[2,16,2048]{2,1,0:T(8,128)(2,1)S(1)}, u32[]{:S(2)}, u32[]{:S(2)}) collective-permute-start(bf16[2,16,2048]{2,1,0:T(8,128)(2,1)} %param.13), channel_id=1, source_target_pairs={{0,128},{128,0},{1,129},{129,1},{2,130},{130,2},{3,131},{131,3},{4... | collective-permute-start | bytes 393224 | tf_op jit(solution)/shard_map/ppermute | solution.py:110
  1.3 4.2 %collective-permute-done.1 = bf16[2,16,2048]{2,1,0:T(8,128)(2,1)S(1)} collective-permute-done((bf16[2,16,2048]{2,1,0:T(8,128)(2,1)}, bf16[2,16,2048]{2,1,0:T(8,128)(2,1)S(1)}, u32[]{:S(2)}, u32[]{:S(2)}) %collective-permute-start.1) | collective-permute-done | bytes 131104 | tf_op jit(solution)/shard_map/ppermute | solution.py:110
  5.5 0.9 broadcast_select_fusion
  6.5 0.7 collective-permute-start.2
  7.1 9.1 %collective-permute-start.3 = (bf16[2,16,2048]{2,1,0:T(8,128)(2,1)S(1)}, bf16[2,16,2048]{2,1,0:T(8,128)(2,1)S(1)}, u32[]{:S(2)}, u32[]{:S(2)}) collective-permute-start(bf16[2,16,2048]{2,1,0:T(8,128)(2,1)S(1)} %get-tuple-element.23), channel_id=1, source_target_pairs={{0,8},{2,40},{4,72},{6,104},{8,0},{10,32},{12,64},{14,96},{32,10},... | collective-permute-start | bytes 393224 | tf_op jit(solution)/shard_map/ppermute | solution.py:126
  16.3 0.6 collective-permute-start.9
  16.8 0.7 convert_element_type.85
  17.5 0.7 convert_element_type.87
  18.2 1.0 %collective-permute-done.3 = bf16[2,16,2048]{2,1,0:T(8,128)(2,1)S(1)} collective-permute-done((bf16[2,16,2048]{2,1,0:T(8,128)(2,1)S(1)}, bf16[2,16,2048]{2,1,0:T(8,128)(2,1)S(1)}, u32[]{:S(2)}, u32[]{:S(2)}) %collective-permute-start.3) | collective-permute-done | bytes 131104 | tf_op jit(solution)/shard_map/ppermute | solution.py:126
  19.3 5.2 %collective-permute-start.4 = (bf16[2,2,16,2048]{3,2,1,0:T(8,128)(2,1)S(1)}, bf16[2,2,16,2048]{3,2,1,0:T(8,128)(2,1)S(1)}, u32[]{:S(2)}, u32[]{:S(2)}) collective-permute-start(bf16[2,2,16,2048]{3,2,1,0:T(8,128)(2,1)S(1)} %pad_maximum_fusion), channel_id=1, source_target_pairs={{0,32},{32,64},{64,96},{96,0},{1,33},{33,65},{65,97},{97,1},{2,34}... | collective-permute-start | bytes 786440 | tf_op jit(solution)/shard_map/ppermute | solution.py:128
  24.4 7.3 %collective-permute-start.5 = (bf16[2,2,16,2048]{3,2,1,0:T(8,128)(2,1)S(1)}, bf16[2,2,16,2048]{3,2,1,0:T(8,128)(2,1)S(1)}, u32[]{:S(2)}, u32[]{:S(2)}) collective-permute-start(bf16[2,2,16,2048]{3,2,1,0:T(8,128)(2,1)S(1)} %pad_maximum_fusion), channel_id=1, source_target_pairs={{0,96},{32,0},{64,32},{96,64},{1,97},{33,1},{65,33},{97,65},{2,98}... | collective-permute-start | bytes 786440 | tf_op jit(solution)/shard_map/ppermute | solution.py:129
  31.7 6.4 %collective-permute-done.4 = bf16[2,2,16,2048]{3,2,1,0:T(8,128)(2,1)S(1)} collective-permute-done((bf16[2,2,16,2048]{3,2,1,0:T(8,128)(2,1)S(1)}, bf16[2,2,16,2048]{3,2,1,0:T(8,128)(2,1)S(1)}, u32[]{:S(2)}, u32[]{:S(2)}) %collective-permute-start.4) | collective-permute-done | bytes 262176 | tf_op jit(solution)/shard_map/ppermute | solution.py:128
  38.1 0.1 collective-permute-start.6
  38.2 3.3 %collective-permute-start.7 = (bf16[1,2,16,2048]{3,2,1,0:T(8,128)(2,1)S(1)}, bf16[1,2,16,2048]{3,2,1,0:T(8,128)(2,1)S(1)}, u32[]{:S(2)}, u32[]{:S(2)}) collective-permute-start(bf16[1,2,16,2048]{3,2,1,0:T(8,128)(2,1)S(1)} %slice.95), channel_id=1, source_target_pairs={{0,96},{32,0},{64,32},{96,64},{1,97},{33,1},{65,33},{97,65},{2,98}... | collective-permute-start | bytes 393224 | tf_op jit(solution)/shard_map/ppermute | solution.py:131
  41.6 2.8 %collective-permute-done.6 = bf16[1,2,16,2048]{3,2,1,0:T(8,128)(2,1)S(1)} collective-permute-done((bf16[1,2,16,2048]{3,2,1,0:T(8,128)(2,1)S(1)}, bf16[1,2,16,2048]{3,2,1,0:T(8,128)(2,1)S(1)}, u32[]{:S(2)}, u32[]{:S(2)}) %collective-permute-start.6) | collective-permute-done | bytes 131104 | tf_op jit(solution)/shard_map/ppermute | solution.py:130
  44.4 0.1 collective-permute-start.8
  44.5 0.1 pad.17.clone
  44.6 0.1 maximum_maximum_fusion.own
  44.7 0.5 collective-permute-start
  45.2 0.1 fusion.17
  45.4 4.5 %collective-permute-done.par = f32[8,20]{1,0:T(8,128)S(1)} collective-permute-done((f32[8,20]{1,0:T(8,128)S(1)}, f32[8,20]{1,0:T(8,128)S(1)}, u32[]{:S(2)}, u32[]{:S(2)}) %collective-permute-start) | collective-permute-done | bytes 672 | tf_op jit(solution)/shard_map/ppermute | solution.py:122
  49.9 0.6 copy-done.5
  50.4 0.5 copy-done.1
  50.9 1.0 copy-done.2
  51.9 7.0 %block_products.1 = (f32[48,128,128]{2,1,0:T(8,128)}, bf16[2,3,128,128]{3,2,1,0:T(8,128)(2,1)}, bf16[2,3,128,128]{3,2,1,0:T(8,128)(2,1)}, bf16[3,128,128]{2,1,0:T(8,128)(2,1)}) custom-call(f32[8,20]{1,0:T(8,128)} %copy-done.4, f32[8,20]{1,0:T(8,128)} %copy-done.5, bf16[8,2,16,2048]{3,2,1,0:T(8,128)(2,1)} %copy-done, bf16[8,2,16,2048]{3,2,1,0:T(8,128)(2,1)} %copy-done.2, ...), custom_call_target="tpu_custom_call" | custom-call | flops 335544320 | bytes 9437184 | tf_op jit(solution)/shard_map/block_products/pallas_call | solution.py:92
  58.9 0.9 collective-permute-start.10
  59.8 5.5 %collective-permute-start.14 = (bf16[2,3,128,128]{3,2,1,0:T(8,128)(2,1)}, bf16[2,3,128,128]{3,2,1,0:T(8,128)(2,1)S(1)}, u32[]{:S(2)}, u32[]{:S(2)}) collective-permute-start(bf16[2,3,128,128]{3,2,1,0:T(8,128)(2,1)} %get-tuple-element.11), channel_id=1, source_target_pairs={{0,14},{2,0},{4,2},{6,4},{8,6},{10,8},{12,10},{14,12},{1,15},{3,1}... | collective-permute-start | bytes 589832 | tf_op jit(solution)/shard_map/ppermute | solution.py:146
  65.3 1.5 %slice_bitcast_fusion.13 = (f32[1,3,128,128]{3,2,1,0:T(8,128)S(1)}, f32[1,3,128,128]{3,2,1,0:T(8,128)S(1)}, f32[1,3,128,128]{3,2,1,0:T(8,128)S(1)}, f32[1,3,128,...) fusion(f32[8,2,3,128,128]{4,3,2,1,0:T(8,128)} %bitcast.96), kind=kLoop, calls=%fused_computation.36 | loop fusion | bytes 2359296 | tf_op jit(solution)/shard_map/stack;squeeze | solution.py:148
  66.8 3.1 %collective-permute-done.10 = bf16[2,3,128,128]{3,2,1,0:T(8,128)(2,1)S(1)} collective-permute-done((bf16[2,3,128,128]{3,2,1,0:T(8,128)(2,1)}, bf16[2,3,128,128]{3,2,1,0:T(8,128)(2,1)S(1)}, u32[]{:S(2)}, u32[]{:S(2)}) %collective-permute-start.10) | collective-permute-done | bytes 196640 | tf_op jit(solution)/shard_map/ppermute | solution.py:145
  69.9 0.1 collective-permute-start.11
  70.1 3.3 %collective-permute-start.15 = (bf16[2,3,128,128]{3,2,1,0:T(8,128)(2,1)S(1)}, bf16[2,3,128,128]{3,2,1,0:T(8,128)(2,1)S(1)}, u32[]{:S(2)}, u32[]{:S(2)}) collective-permute-start(bf16[2,3,128,128]{3,2,1,0:T(8,128)(2,1)S(1)} %fusion.4), channel_id=1, source_target_pairs={{0,14},{2,0},{4,2},{6,4},{8,6},{10,8},{12,10},{14,12},{1,15},{3,1}... | collective-permute-start | bytes 589832 | tf_op jit(solution)/shard_map/ppermute | solution.py:151
  73.4 3.5 %collective-permute-done.11 = bf16[2,3,128,128]{3,2,1,0:T(8,128)(2,1)S(1)} collective-permute-done((bf16[2,3,128,128]{3,2,1,0:T(8,128)(2,1)S(1)}, bf16[2,3,128,128]{3,2,1,0:T(8,128)(2,1)S(1)}, u32[]{:S(2)}, u32[]{:S(2)}) %collective-permute-start.11) | collective-permute-done | bytes 196640 | tf_op jit(solution)/shard_map/ppermute | solution.py:150
  76.9 1.1 %fusion.9 = (bf16[3,128,128]{2,1,0:T(8,128)(2,1)S(1)}, bf16[3,128,128]{2,1,0:T(8,128)(2,1)S(1)}) fusion(f32[8,2,3,128,128]{4,3,2,1,0:T(8,128)} %bitcast.97, f32[2,3,128,128]{3,2,1,0:T(8,128)S(1)} %convert_element_type.95), kind=kLoop, calls=%fused_computation.19 | loop fusion | flops 196608 | bytes 983040 | tf_op jit(solution)/shard_map/convert_element_type | solution.py:139
  78.0 0.1 collective-permute-start.12
  78.1 0.1 fusion.5
  78.1 3.5 %collective-permute-start.16 = (bf16[2,3,128,128]{3,2,1,0:T(8,128)(2,1)S(1)}, bf16[2,3,128,128]{3,2,1,0:T(8,128)(2,1)S(1)}, u32[]{:S(2)}, u32[]{:S(2)}) collective-permute-start(bf16[2,3,128,128]{3,2,1,0:T(8,128)(2,1)S(1)} %fusion.5), channel_id=1, source_target_pairs={{0,14},{2,0},{4,2},{6,4},{8,6},{10,8},{12,10},{14,12},{1,15},{3,1}... | collective-permute-start | bytes 589832 | tf_op jit(solution)/shard_map/ppermute | solution.py:156
  81.6 2.3 %collective-permute-done.12 = bf16[3,128,128]{2,1,0:T(8,128)(2,1)S(1)} collective-permute-done((bf16[3,128,128]{2,1,0:T(8,128)(2,1)S(1)}, bf16[3,128,128]{2,1,0:T(8,128)(2,1)S(1)}, u32[]{:S(2)}, u32[]{:S(2)}) %collective-permute-start.12) | collective-permute-done | bytes 98336 | tf_op jit(solution)/shard_map/ppermute | solution.py:155
  83.9 1.0 fusion.13
  84.8 0.1 collective-permute-start.13
  85.0 0.6 collective-permute-start.17
  85.6 1.2 %collective-permute-start.18 = (bf16[3,128,128]{2,1,0:T(8,128)(2,1)S(1)}, bf16[3,128,128]{2,1,0:T(8,128)(2,1)S(1)}, u32[]{:S(2)}, u32[]{:S(2)}) collective-permute-start(bf16[3,128,128]{2,1,0:T(8,128)(2,1)S(1)} %get-tuple-element.13), channel_id=1, source_target_pairs={{0,3},{1,2},{2,5},{3,4},{4,7},{5,6},{6,9},{7,8},{8,11},{9,10},{10,... | collective-permute-start | bytes 294920 | tf_op jit(solution)/shard_map/ppermute | solution.py:157
  86.9 3.9 %collective-permute-done.13 = bf16[3,128,128]{2,1,0:T(8,128)(2,1)S(1)} collective-permute-done((bf16[3,128,128]{2,1,0:T(8,128)(2,1)S(1)}, bf16[3,128,128]{2,1,0:T(8,128)(2,1)S(1)}, u32[]{:S(2)}, u32[]{:S(2)}) %collective-permute-start.13) | collective-permute-done | bytes 98336 | tf_op jit(solution)/shard_map/ppermute | solution.py:158
  90.8 1.1 %fusion.7 = (bf16[3,128,128]{2,1,0:T(8,128)(2,1)S(1)}, bf16[3,128,128]{2,1,0:T(8,128)(2,1)S(1)}) fusion(f32[8,2,3,128,128]{4,3,2,1,0:T(8,128)} %bitcast.99, f32[2,3,128,128]{3,2,1,0:T(8,128)S(1)} %convert_element_type.104, bf16[3,128,128]{2,1,0:T(8,128)(2,1)S(1)} %collective-permute-done.13), kind=kLoop, calls=%fused_computation.15 | loop fusion | flops 294912 | bytes 1081344 | tf_op jit(solution)/shard_map/convert_element_type | solution.py:139
  91.8 0.6 collective-permute-start.19
  92.5 0.2 fusion.18
  92.7 1.7 %collective-permute-done.18 = bf16[3,128,128]{2,1,0:T(8,128)(2,1)S(1)} collective-permute-done((bf16[3,128,128]{2,1,0:T(8,128)(2,1)S(1)}, bf16[3,128,128]{2,1,0:T(8,128)(2,1)S(1)}, u32[]{:S(2)}, u32[]{:S(2)}) %collective-permute-start.18) | collective-permute-done | bytes 98336 | tf_op jit(solution)/shard_map/ppermute | solution.py:157
  94.3 4.6 %collective-permute-done.19 = bf16[3,128,128]{2,1,0:T(8,128)(2,1)S(1)} collective-permute-done((bf16[3,128,128]{2,1,0:T(8,128)(2,1)S(1)}, bf16[3,128,128]{2,1,0:T(8,128)(2,1)S(1)}, u32[]{:S(2)}, u32[]{:S(2)}) %collective-permute-start.19) | collective-permute-done | bytes 98336 | tf_op jit(solution)/shard_map/ppermute | solution.py:159
  99.0 0.9 fusion.2
  (45 shorter events, 0.4 us)
Async XLA Ops:
  0.0 44.5 %copy-start.8 = (s32[2,1,1]{0,2,1:T(1,128)S(1)}, s32[2,1,1]{0,2,1:T(1,128)}, u32[]{:S(2)}) copy-start(s32[2,1,1]{0,2,1:T(1,128)} %param.11) | copy-start | bytes 28
  0.0 44.6 %copy-start.9 = (bf16[2,1,1,20]{3,0,2,1:T(2,128)(2,1)S(1)}, bf16[2,1,1,20]{3,0,2,1:T(2,128)(2,1)}, u32[]{:S(2)}) copy-start(bf16[2,1,1,20]{3,0,2,1:T(2,128)(2,1)} %param.12) | copy-start | bytes 244
  0.0 45.2 %copy-start.3 = (bf16[256,256]{1,0:T(8,128)(2,1)S(1)}, bf16[256,256]{1,0:T(8,128)(2,1)}, u32[]{:S(2)}) copy-start(bf16[256,256]{1,0:T(8,128)(2,1)} %param.14) | copy-start | bytes 393220
  0.0 5.5 %collective-permute-start.1 = (bf16[2,16,2048]{2,1,0:T(8,128)(2,1)}, bf16[2,16,2048]{2,1,0:T(8,128)(2,1)S(1)}, u32[]{:S(2)}, u32[]{:S(2)}) collective-permute-start(bf16[2,16,2048]{2,1,0:T(8,128)(2,1)} %param.13), channel_id=1, source_target_pairs={{0,128},{128,0},{1,129},{129,1},{2,130},{130,2},{3,131},{131,3},{4... | collective-permute-start | bytes 393224 | tf_op jit(solution)/shard_map/ppermute | solution.py:110
  6.5 11.7 %collective-permute-start.2 = (bf16[2,16,2048]{2,1,0:T(8,128)(2,1)S(1)}, bf16[2,16,2048]{2,1,0:T(8,128)(2,1)S(1)}, u32[]{:S(2)}, u32[]{:S(2)}) collective-permute-start(bf16[2,16,2048]{2,1,0:T(8,128)(2,1)S(1)} %get-tuple-element.24), channel_id=1, source_target_pairs={{0,0},{2,32},{4,64},{6,96},{8,8},{10,40},{12,72},{14,104},{32,2},{... | collective-permute-start | bytes 393224 | tf_op jit(solution)/shard_map/ppermute | solution.py:125
  7.1 12.1 %collective-permute-start.3 = (bf16[2,16,2048]{2,1,0:T(8,128)(2,1)S(1)}, bf16[2,16,2048]{2,1,0:T(8,128)(2,1)S(1)}, u32[]{:S(2)}, u32[]{:S(2)}) collective-permute-start(bf16[2,16,2048]{2,1,0:T(8,128)(2,1)S(1)} %get-tuple-element.23), channel_id=1, source_target_pairs={{0,8},{2,40},{4,72},{6,104},{8,0},{10,32},{12,64},{14,96},{32,10},... | collective-permute-start | bytes 393224 | tf_op jit(solution)/shard_map/ppermute | solution.py:126
  16.3 33.6 %collective-permute-start.9 = (bf16[40,128,128]{2,1,0:T(8,128)(2,1)}, bf16[40,128,128]{2,1,0:T(8,128)(2,1)S(1)}, u32[]{:S(2)}, u32[]{:S(2)}) collective-permute-start(bf16[40,128,128]{2,1,0:T(8,128)(2,1)} %bitcast.100), channel_id=1, source_target_pairs={{0,1},{1,0},{2,3},{3,2},{4,5},{5,4},{6,7},{7,6},{8,9},{9,8},{10,11... | collective-permute-start | bytes 3932168 | tf_op jit(solution)/shard_map/ppermute | solution.py:112
  19.3 18.8 %collective-permute-start.4 = (bf16[2,2,16,2048]{3,2,1,0:T(8,128)(2,1)S(1)}, bf16[2,2,16,2048]{3,2,1,0:T(8,128)(2,1)S(1)}, u32[]{:S(2)}, u32[]{:S(2)}) collective-permute-start(bf16[2,2,16,2048]{3,2,1,0:T(8,128)(2,1)S(1)} %pad_maximum_fusion), channel_id=1, source_target_pairs={{0,32},{32,64},{64,96},{96,0},{1,33},{33,65},{65,97},{97,1},{2,34}... | collective-permute-start | bytes 786440 | tf_op jit(solution)/shard_map/ppermute | solution.py:128
  24.4 13.8 %collective-permute-start.5 = (bf16[2,2,16,2048]{3,2,1,0:T(8,128)(2,1)S(1)}, bf16[2,2,16,2048]{3,2,1,0:T(8,128)(2,1)S(1)}, u32[]{:S(2)}, u32[]{:S(2)}) collective-permute-start(bf16[2,2,16,2048]{3,2,1,0:T(8,128)(2,1)S(1)} %pad_maximum_fusion), channel_id=1, source_target_pairs={{0,96},{32,0},{64,32},{96,64},{1,97},{33,1},{65,33},{97,65},{2,98}... | collective-permute-start | bytes 786440 | tf_op jit(solution)/shard_map/ppermute | solution.py:129
  38.1 6.3 %collective-permute-start.6 = (bf16[1,2,16,2048]{3,2,1,0:T(8,128)(2,1)S(1)}, bf16[1,2,16,2048]{3,2,1,0:T(8,128)(2,1)S(1)}, u32[]{:S(2)}, u32[]{:S(2)}) collective-permute-start(bf16[1,2,16,2048]{3,2,1,0:T(8,128)(2,1)S(1)} %slice.94), channel_id=1, source_target_pairs={{0,32},{32,64},{64,96},{96,0},{1,33},{33,65},{65,97},{97,1},{2,34}... | collective-permute-start | bytes 393224 | tf_op jit(solution)/shard_map/ppermute | solution.py:130
  38.2 6.2 %collective-permute-start.7 = (bf16[1,2,16,2048]{3,2,1,0:T(8,128)(2,1)S(1)}, bf16[1,2,16,2048]{3,2,1,0:T(8,128)(2,1)S(1)}, u32[]{:S(2)}, u32[]{:S(2)}) collective-permute-start(bf16[1,2,16,2048]{3,2,1,0:T(8,128)(2,1)S(1)} %slice.95), channel_id=1, source_target_pairs={{0,96},{32,0},{64,32},{96,64},{1,97},{33,1},{65,33},{97,65},{2,98}... | collective-permute-start | bytes 393224 | tf_op jit(solution)/shard_map/ppermute | solution.py:131
  44.4 5.5 %copy-start = (bf16[8,2,16,2048]{3,2,1,0:T(8,128)(2,1)}, bf16[8,2,16,2048]{3,2,1,0:T(8,128)(2,1)S(1)}, u32[]{:S(2)}) copy-start(bf16[8,2,16,2048]{3,2,1,0:T(8,128)(2,1)S(1)} %constant_dynamic-update-slice_fusion.feats0) | copy-start | bytes 3145732
  44.4 5.4 %collective-permute-start.8 = (bf16[8,2,16,2048]{3,2,1,0:T(8,128)(2,1)S(1)}, bf16[8,2,16,2048]{3,2,1,0:T(8,128)(2,1)S(1)}, u32[]{:S(2)}, u32[]{:S(2)}) collective-permute-start(bf16[8,2,16,2048]{3,2,1,0:T(8,128)(2,1)S(1)} %constant_dynamic-update-slice_fusion.feats0), channel_id=1, source_target_pairs={{0,16},{16,0},{1,17},{17,1},{2,18},{18,2},{3,19},{19,3},{4,20},{20... | collective-permute-start | bytes 3145736 | tf_op jit(solution)/shard_map/ppermute | solution.py:133
  44.7 5.2 %copy-start.4 = (f32[8,20]{1,0:T(8,128)}, f32[8,20]{1,0:T(8,128)S(1)}, u32[]{:S(2)}) copy-start(f32[8,20]{1,0:T(8,128)S(1)} %maximum_maximum_fusion.own) | copy-start | bytes 1924
  44.7 5.1 %collective-permute-start = (f32[8,20]{1,0:T(8,128)S(1)}, f32[8,20]{1,0:T(8,128)S(1)}, u32[]{:S(2)}, u32[]{:S(2)}) collective-permute-start(f32[8,20]{1,0:T(8,128)S(1)} %maximum_maximum_fusion.own), channel_id=1, source_target_pairs={{0,1},{1,0},{2,3},{3,2},{4,5},{5,4},{6,7},{7,6},{8,9},{9,8},{10,11... | collective-permute-start | bytes 1928 | tf_op jit(solution)/shard_map/ppermute | solution.py:122
  49.8 0.6 copy-start.5
  49.8 1.1 %copy-start.1 = (bf16[40,128,128]{2,1,0:T(8,128)(2,1)}, bf16[40,128,128]{2,1,0:T(8,128)(2,1)S(1)}, u32[]{:S(2)}) copy-start(bf16[40,128,128]{2,1,0:T(8,128)(2,1)S(1)} %collective-permute-done.9.adj_par) | copy-start | bytes 3932164
  50.9 1.0 copy-start.2
  58.9 10.9 %collective-permute-start.10 = (bf16[2,3,128,128]{3,2,1,0:T(8,128)(2,1)}, bf16[2,3,128,128]{3,2,1,0:T(8,128)(2,1)S(1)}, u32[]{:S(2)}, u32[]{:S(2)}) collective-permute-start(bf16[2,3,128,128]{3,2,1,0:T(8,128)(2,1)} %get-tuple-element.10), channel_id=1, source_target_pairs={{0,2},{2,4},{4,6},{6,8},{8,10},{10,12},{12,14},{14,0},{1,3},{3,5},... | collective-permute-start | bytes 589832 | tf_op jit(solution)/shard_map/ppermute | solution.py:145
  59.8 10.2 %collective-permute-start.14 = (bf16[2,3,128,128]{3,2,1,0:T(8,128)(2,1)}, bf16[2,3,128,128]{3,2,1,0:T(8,128)(2,1)S(1)}, u32[]{:S(2)}, u32[]{:S(2)}) collective-permute-start(bf16[2,3,128,128]{3,2,1,0:T(8,128)(2,1)} %get-tuple-element.11), channel_id=1, source_target_pairs={{0,14},{2,0},{4,2},{6,4},{8,6},{10,8},{12,10},{14,12},{1,15},{3,1}... | collective-permute-start | bytes 589832 | tf_op jit(solution)/shard_map/ppermute | solution.py:146
  65.3 19.6 %copy-start.7 = (bf16[3,128,128]{2,1,0:T(8,128)(2,1)S(1)}, bf16[3,128,128]{2,1,0:T(8,128)(2,1)}, u32[]{:S(2)}) copy-start(bf16[3,128,128]{2,1,0:T(8,128)(2,1)} %get-tuple-element.12) | copy-start | bytes 294916
  69.9 7.0 %collective-permute-start.11 = (bf16[2,3,128,128]{3,2,1,0:T(8,128)(2,1)S(1)}, bf16[2,3,128,128]{3,2,1,0:T(8,128)(2,1)S(1)}, u32[]{:S(2)}, u32[]{:S(2)}) collective-permute-start(bf16[2,3,128,128]{3,2,1,0:T(8,128)(2,1)S(1)} %fusion.3), channel_id=1, source_target_pairs={{0,2},{2,4},{4,6},{6,8},{8,10},{10,12},{12,14},{14,0},{1,3},{3,5},... | collective-permute-start | bytes 589832 | tf_op jit(solution)/shard_map/ppermute | solution.py:150
  70.0 29.0 %copy-start.6 = (f32[256]{0:T(256)S(1)}, f32[256]{0:T(256)}, u32[]{:S(2)}) copy-start(f32[256]{0:T(256)} %param.15) | copy-start | bytes 3076
  70.1 8.0 %collective-permute-start.15 = (bf16[2,3,128,128]{3,2,1,0:T(8,128)(2,1)S(1)}, bf16[2,3,128,128]{3,2,1,0:T(8,128)(2,1)S(1)}, u32[]{:S(2)}, u32[]{:S(2)}) collective-permute-start(bf16[2,3,128,128]{3,2,1,0:T(8,128)(2,1)S(1)} %fusion.4), channel_id=1, source_target_pairs={{0,14},{2,0},{4,2},{6,4},{8,6},{10,8},{12,10},{14,12},{1,15},{3,1}... | collective-permute-start | bytes 589832 | tf_op jit(solution)/shard_map/ppermute | solution.py:151
  78.0 5.9 %collective-permute-start.12 = (bf16[3,128,128]{2,1,0:T(8,128)(2,1)S(1)}, bf16[3,128,128]{2,1,0:T(8,128)(2,1)S(1)}, u32[]{:S(2)}, u32[]{:S(2)}) collective-permute-start(bf16[3,128,128]{2,1,0:T(8,128)(2,1)S(1)} %get-tuple-element.14), channel_id=1, source_target_pairs={{0,2},{2,4},{4,6},{6,8},{8,10},{10,12},{12,14},{14,0},{1,3},{3,5},... | collective-permute-start | bytes 294920 | tf_op jit(solution)/shard_map/ppermute | solution.py:155
  78.1 8.7 %collective-permute-start.16 = (bf16[2,3,128,128]{3,2,1,0:T(8,128)(2,1)S(1)}, bf16[2,3,128,128]{3,2,1,0:T(8,128)(2,1)S(1)}, u32[]{:S(2)}, u32[]{:S(2)}) collective-permute-start(bf16[2,3,128,128]{3,2,1,0:T(8,128)(2,1)S(1)} %fusion.5), channel_id=1, source_target_pairs={{0,14},{2,0},{4,2},{6,4},{8,6},{10,8},{12,10},{14,12},{1,15},{3,1}... | collective-permute-start | bytes 589832 | tf_op jit(solution)/shard_map/ppermute | solution.py:156
  84.8 5.9 %collective-permute-start.13 = (bf16[3,128,128]{2,1,0:T(8,128)(2,1)S(1)}, bf16[3,128,128]{2,1,0:T(8,128)(2,1)S(1)}, u32[]{:S(2)}, u32[]{:S(2)}) collective-permute-start(bf16[3,128,128]{2,1,0:T(8,128)(2,1)S(1)} %fusion.13), channel_id=1, source_target_pairs={{0,2},{2,4},{4,6},{6,8},{8,10},{10,12},{12,14},{14,0},{1,3},{3,5},... | collective-permute-start | bytes 294920 | tf_op jit(solution)/shard_map/ppermute | solution.py:158
  85.0 7.7 %collective-permute-start.17 = (bf16[3,128,128]{2,1,0:T(8,128)(2,1)S(1)}, bf16[3,128,128]{2,1,0:T(8,128)(2,1)S(1)}, u32[]{:S(2)}, u32[]{:S(2)}) collective-permute-start(bf16[3,128,128]{2,1,0:T(8,128)(2,1)S(1)} %copy-done.7), channel_id=1, source_target_pairs={{0,1},{1,0},{2,3},{3,2},{4,5},{5,4},{6,7},{7,6},{8,9},{9,8},{10,11... | collective-permute-start | bytes 294920 | tf_op jit(solution)/shard_map/ppermute | solution.py:147
  85.6 8.7 %collective-permute-start.18 = (bf16[3,128,128]{2,1,0:T(8,128)(2,1)S(1)}, bf16[3,128,128]{2,1,0:T(8,128)(2,1)S(1)}, u32[]{:S(2)}, u32[]{:S(2)}) collective-permute-start(bf16[3,128,128]{2,1,0:T(8,128)(2,1)S(1)} %get-tuple-element.13), channel_id=1, source_target_pairs={{0,3},{1,2},{2,5},{3,4},{4,7},{5,6},{6,9},{7,8},{8,11},{9,10},{10,... | collective-permute-start | bytes 294920 | tf_op jit(solution)/shard_map/ppermute | solution.py:157
  91.8 7.1 %collective-permute-start.19 = (bf16[3,128,128]{2,1,0:T(8,128)(2,1)S(1)}, bf16[3,128,128]{2,1,0:T(8,128)(2,1)S(1)}, u32[]{:S(2)}, u32[]{:S(2)}) collective-permute-start(bf16[3,128,128]{2,1,0:T(8,128)(2,1)S(1)} %get-tuple-element.15), channel_id=1, source_target_pairs={{0,15},{1,14},{2,1},{3,0},{4,3},{5,2},{6,5},{7,4},{8,7},{9,6},{10,... | collective-permute-start | bytes 294920 | tf_op jit(solution)/shard_map/ppermute | solution.py:159
where the time goes:
time: 101 us; the launch traced here: 99.9 us
  starting transfers between devices  43.9 us (43%)
  waiting for transfers between devices  38 us (38%)
  Pallas kernels  7.02 us (7%)
  other arithmetic  5.84 us (6%)
  local copies, waits for them, and re-layouts  3.69 us (4%)
  matrix products  1.06 us (1%)
    ppermute x3, starting transfers between devices, body(): got_b = full(lax.ppermute(bwd, 'z', back))  12.3 us
    ppermute x1, starting transfers between devices, body(): lax.ppermute(jnp.where(low_plane, swapped, features), ('xl', 'y', 'z'), t...  9.1 us
    ppermute x3, waiting for transfers between devices, body(): got_f = full(lax.ppermute(fwd, 'z', ahead))  8.86 us
    ppermute x1, starting transfers between devices, body(): above = lax.ppermute(here, 'y', shift(4, -1))  7.26 us
    pallas_call x1, Pallas kernels, block_products(): pl.pallas_call(block_kernel, out_shape=(jax.ShapeDtypeStruct((ROWS, BS, H...  7.02 us
    ppermute x1, waiting for transfers between devices, body(): below = lax.ppermute(here, 'y', shift(4, 1))  6.37 us
    ppermute x1, starting transfers between devices, body(): below = lax.ppermute(here, 'y', shift(4, 1))  5.16 us
    ppermute x1, waiting for transfers between devices, body(): lax.ppermute(low(got_b[0] + part[7, 1]), COL, shift_and_cross(-1))  4.62 us
  transfers between devices with their start and end apart: 20, of which 11 were waited for; matrix products, arithmetic and copies ran while one was open for 7% of the time, Pallas kernels for 0%

commit v1 on v0

--- a/solution.py
+++ b/solution.py
@@ -36,7 +36,7 @@
     return pairs
 
 
-def block_kernel(own, par, feats0, feats1, adj_own, adj_par, part, fwd, bwd, cross):
+def block_kernel(own, par, feats0, feats1, adj_own, adj_par, keep0, keep2, keep6, msg1, msg3, msg5, msg7, msg4a, msg4b, part):
     core, xl = lax.axis_index("core"), lax.axis_index("xl")
     z, xh = lax.axis_index("z"), lax.axis_index("xh")
     flip = jnp.where(xl == z // 4, 0, 1)
@@ -61,8 +61,9 @@
                     slot = g * GROUP + u
                     row = table[t, slot].astype(jnp.int32)
                     stop = (row // 6 - z) & (NZ - 1)
-                    place = stop * 6 + (((row // 3) & 1) ^ xh) * 3 + row % 3
+                    half = ((row // 3) & 1) ^ xh
                     scale = jnp.where(slot < live, table[4 + t, slot], 0.0)
+                    place = stop * 6 + half * 3 + row % 3
                     part[place] = part[place] + prods[u] * scale
                 return carry
 
@@ -78,27 +79,26 @@
         run(feats1, adj_own, own)
         run(feats0, adj_par, par)
 
-    for i, place in enumerate((24, 21)):
-        fwd[i] = part[pl.ds(place, 3)].astype(fwd.dtype)
-    for i, place in enumerate((27, 30)):
-        bwd[i] = part[pl.ds(place, 3)].astype(bwd.dtype)
-    cross[...] = part[pl.ds(3, 3)].astype(cross.dtype)
+    for ref, stop in ((msg3, 3), (msg5, 5), (msg1, 1), (msg7, 7), (keep2, 2), (keep6, 6), (keep0, 0)):
+        for half in range(2):
+            ref[half] = part[pl.ds(stop * 6 + half * 3, 3)].astype(ref.dtype)
+    for ref, half in ((msg4a, 0), (msg4b, 1)):
+        ref[...] = part[pl.ds(24 + half * 3, 3)].astype(ref.dtype)
 
 
 def block_products(own, par, feats0, feats1, adj_own, adj_par):
     smem = pl.BlockSpec(memory_space=pltpu.SMEM)
     vmem = pl.BlockSpec(memory_space=pltpu.VMEM)
+    keep = jax.ShapeDtypeStruct((2, 3, BS, HALF), jnp.float32)
     message = jax.ShapeDtypeStruct((2, 3, BS, HALF), jnp.bfloat16)
+    single = jax.ShapeDtypeStruct((3, BS, HALF), jnp.bfloat16)
     return pl.pallas_call(
         block_kernel,
-        out_shape=(
-            jax.ShapeDtypeStruct((ROWS, BS, HALF), jnp.float32),
-            message,
-            message,
-            jax.ShapeDtypeStruct((3, BS, HALF), jnp.bfloat16),
-        ),
+        out_shape=(keep,) * 3 + (message,) * 4 + (single,) * 2,
         in_specs=[smem, smem, vmem, vmem, vmem, vmem],
-        out_specs=(vmem, vmem, vmem, vmem),
+        out_specs=(vmem,) * 9,
+        scratch_shapes=[pltpu.VMEM((ROWS, BS, HALF), jnp.float32)],
+        compiler_params=pltpu.CompilerParams(vmem_limit_bytes=16 << 20),
         cost_estimate=pl.CostEstimate(flops=80 * 2 * BS**3, bytes_accessed=9 << 20, transcendentals=0),
         name="block_products",
     )(own, par, feats0, feats1, adj_own, adj_par)
@@ -108,8 +108,6 @@
     y = lax.axis_index("y")
     z, xh = (lax.axis_index(a) for a in COL)
     swapped = lax.ppermute(features, "xl", SWAP)
-    adj = adj_values.reshape(STEPS * MAXB, BS, BS)
-    adj_par = lax.ppermute(adj, "xh", SWAP)
     slots = (STEPS, MAXB)
     table = jnp.concatenate(
         [
@@ -120,11 +118,13 @@
         ]
     )
     table_par = lax.ppermute(table, "xh", SWAP)
+    adj = adj_values.reshape(STEPS * MAXB, BS, BS)
+    adj_par = lax.ppermute(adj, "xh", SWAP)
 
     low_plane = z < 4
     first = lax.ppermute(jnp.where(low_plane, features, swapped), ("xl", "y", "z"), to_plane(0))
     second = lax.ppermute(jnp.where(low_plane, swapped, features), ("xl", "y", "z"), to_plane(1))
-    here = jnp.stack([first, second])
+    here, table, table_par = lax.optimization_barrier((jnp.stack([first, second]), table, table_par))
     below = lax.ppermute(here, "y", shift(4, 1))
     above = lax.ppermute(here, "y", shift(4, -1))
     far0 = lax.ppermute(below[:1], "y", shift(4, 1))
@@ -132,8 +132,9 @@
     feats0 = jnp.concatenate([here, below, above, far0, far1])
     feats1 = lax.ppermute(feats0, "core", SWAP)
 
-    part, fwd, bwd, cross = block_products(table, table_par, feats0, feats1, adj, adj_par)
-    part = part.reshape(NZ, 2, 3, BS, HALF)
+    keep0, keep2, keep6, msg1, msg3, msg5, msg7, msg4a, msg4b = block_products(
+        table, table_par, feats0, feats1, adj, adj_par
+    )
 
     def low(v):
         return v.astype(jnp.bfloat16)
@@ -141,24 +142,22 @@
     def full(v):
         return v.astype(jnp.float32)
 
-    ahead, back = shift(NZ, 1), shift(NZ, -1)
-    got_f = full(lax.ppermute(fwd, "z", ahead))
-    got_b = full(lax.ppermute(bwd, "z", back))
-    crossed = full(lax.ppermute(cross, "xh", SWAP))
-    fwd = low(got_f + jnp.stack([part[3, 0], part[2, 1]]))
-    bwd = low(got_b + jnp.stack([part[5, 1], part[6, 0]]))
-    got_f = full(lax.ppermute(fwd, "z", ahead))
-    got_b = full(lax.ppermute(bwd, "z", back))
-    fwd = low(got_f[0] + part[2, 0])
-    fwd_cross = low(got_f[1] + part[1, 1])
-    bwd = low(got_b + jnp.stack([part[6, 1], part[7, 0]]))
-    got_f = full(lax.ppermute(fwd, "z", ahead))
-    got_b = full(lax.ppermute(bwd, "z", back))
-    crossed_f = full(lax.ppermute(fwd_cross, COL, shift_and_cross(1)))
-    last_f = full(lax.ppermute(low(got_f + part[1, 0]), "z", ahead))
-    crossed_b = full(lax.ppermute(low(got_b[0] + part[7, 1]), COL, shift_and_cross(-1)))
-    mine = low(part[0, 0] + last_f + got_b[1])
-    other = low(crossed + crossed_f + crossed_b)
+    def along(v, by):
+        return full(lax.ppermute(v, "z", shift(NZ, by)))
+
+    def across(v, by):
+        return full(lax.ppermute(v, COL, shift_and_cross(by)))
+
+    got3, got5 = along(msg3, 1), along(msg5, -1)
+    got4a, got4b = along(msg4a, 2), along(msg4b, -2)
+    got1, got7 = along(msg1, 1), along(msg7, -1)
+    ahead_mine = along(low(keep2[0] + got3[0] + got4a), 2)
+    back_mine = along(low(keep6[0] + got5[0]), -2)
+    ahead_cross = across(low(keep2[1] + got3[1]), 2)
+    back_cross = across(low(keep6[1] + got5[1] + got4b), -2)
+    near_cross = full(lax.ppermute(low(keep0[1] + got1[1] + got7[1]), "xh", SWAP))
+    mine = low(keep0[0] + got1[0] + got7[0] + ahead_mine + back_mine)
+    other = low(near_cross + ahead_cross + back_cross)
 
     w = weight.reshape(2, 4, 2, 16, 256)
     w = jnp.concatenate([w, w], axis=1)
@@ -183,4 +182,5 @@
         P(),
         P(),
     )
+
     return jax.shard_map(body, mesh=split, in_specs=in_specs, out_specs=P(ROW + COL, None), check_vma=False)

time: 101 us -> 103 us (1.020)
  the two profiles are of different devices: /device:TPU:4 before, /device:TPU:12 now
where the time goes in v1:
time: 103 us; the launch traced here: 101 us
  starting transfers between devices  48.5 us (47%)
  waiting for transfers between devices  42.8 us (42%)
  Pallas kernels  4.38 us (4%)
  other arithmetic  4.17 us (4%)
  matrix products  1.05 us (1%)
    ppermute x8, starting transfers between devices, along(): return full(lax.ppermute(v, 'z', shift(NZ, by)))  17.5 us
    ppermute x1, waiting for transfers between devices, body(): adj_par = lax.ppermute(adj, 'xh', SWAP)  16 us
    ppermute x8, waiting for transfers between devices, along(): return full(lax.ppermute(v, 'z', shift(NZ, by)))  11.4 us
    ppermute x1, starting transfers between devices, body(): lax.ppermute(jnp.where(low_plane, swapped, features), ('xl', 'y', 'z'), t...  8.76 us
    ppermute x2, starting transfers between devices, across(): return full(lax.ppermute(v, COL, shift_and_cross(by)))  6.67 us
    ppermute x1, waiting for transfers between devices, body(): below = lax.ppermute(here, 'y', shift(4, 1))  4.82 us
    ppermute x1, starting transfers between devices, body(): far0 = lax.ppermute(below[:1], 'y', shift(4, 1))  4.68 us
    pallas_call x1, Pallas kernels, block_products(): pl.pallas_call(block_kernel, out_shape=(keep,) * 3 + (message,) * 4 + (si...  4.38 us
  transfers between devices with their start and end apart: 21, of which 14 were waited for; matrix products, arithmetic and copies ran while one was open for 3% of the time, Pallas kernels for 0%

profile of v1, /device:TPU:12, one launch (start us, length us, event | category | flops | bytes accessed | tf_op | source)
XLA Modules:
  0.0 101.4 jit_solution(8498917010624400524)
XLA Ops:
  0.0 1.2 %collective-permute-start = (bf16[2,16,2048]{2,1,0:T(8,128)(2,1)}, bf16[2,16,2048]{2,1,0:T(8,128)(2,1)S(1)}, u32[]{:S(2)}, u32[]{:S(2)}) collective-permute-start(bf16[2,16,2048]{2,1,0:T(8,128)(2,1)} %param.13), channel_id=1, source_target_pairs={{0,128},{128,0},{1,129},{129,1},{2,130},{130,2},{3,131},{131,3},{4... | collective-permute-start | bytes 393224 | tf_op jit(solution)/shard_map/ppermute | solution.py:110
  1.2 0.7 convert_element_type.91
  1.9 0.7 convert_element_type.93
  2.6 0.7 convert_bitcast_fusion
  3.2 0.1 pad.9.clone
  3.3 0.7 bitcast_convert_fusion
  4.0 1.5 %collective-permute-done = bf16[2,16,2048]{2,1,0:T(8,128)(2,1)S(1)} collective-permute-done((bf16[2,16,2048]{2,1,0:T(8,128)(2,1)}, bf16[2,16,2048]{2,1,0:T(8,128)(2,1)S(1)}, u32[]{:S(2)}, u32[]{:S(2)}) %collective-permute-start) | collective-permute-done | bytes 131104 | tf_op jit(solution)/shard_map/ppermute | solution.py:110
  5.4 0.9 broadcast_select_fusion.1
  6.4 3.7 %collective-permute-start.1 = (bf16[2,16,2048]{2,1,0:T(8,128)(2,1)S(1)}, bf16[2,16,2048]{2,1,0:T(8,128)(2,1)S(1)}, u32[]{:S(2)}, u32[]{:S(2)}) collective-permute-start(bf16[2,16,2048]{2,1,0:T(8,128)(2,1)S(1)} %get-tuple-element.29), channel_id=1, source_target_pairs={{0,0},{2,32},{4,64},{6,96},{8,8},{10,40},{12,72},{14,104},{32,2},{... | collective-permute-start | bytes 393224 | tf_op jit(solution)/shard_map/ppermute | solution.py:125
  10.1 8.8 %collective-permute-start.2 = (bf16[2,16,2048]{2,1,0:T(8,128)(2,1)S(1)}, bf16[2,16,2048]{2,1,0:T(8,128)(2,1)S(1)}, u32[]{:S(2)}, u32[]{:S(2)}) collective-permute-start(bf16[2,16,2048]{2,1,0:T(8,128)(2,1)S(1)} %get-tuple-element.30), channel_id=1, source_target_pairs={{0,8},{2,40},{4,72},{6,104},{8,0},{10,32},{12,64},{14,96},{32,10},... | collective-permute-start | bytes 393224 | tf_op jit(solution)/shard_map/ppermute | solution.py:126
  18.9 0.1 maximum_maximum_fusion.own
  18.9 0.5 collective-permute-start.3
  19.5 1.1 %collective-permute-done.1 = bf16[2,16,2048]{2,1,0:T(8,128)(2,1)S(1)} collective-permute-done((bf16[2,16,2048]{2,1,0:T(8,128)(2,1)S(1)}, bf16[2,16,2048]{2,1,0:T(8,128)(2,1)S(1)}, u32[]{:S(2)}, u32[]{:S(2)}) %collective-permute-start.1) | collective-permute-done | bytes 131104 | tf_op jit(solution)/shard_map/ppermute | solution.py:125
  20.5 2.1 %collective-permute-done.2 = bf16[2,16,2048]{2,1,0:T(8,128)(2,1)S(1)} collective-permute-done((bf16[2,16,2048]{2,1,0:T(8,128)(2,1)S(1)}, bf16[2,16,2048]{2,1,0:T(8,128)(2,1)S(1)}, u32[]{:S(2)}, u32[]{:S(2)}) %collective-permute-start.2) | collective-permute-done | bytes 131104 | tf_op jit(solution)/shard_map/ppermute | solution.py:126
  22.7 1.4 %collective-permute-done.3.par = f32[8,20]{1,0:T(8,128)S(1)} collective-permute-done((f32[8,20]{1,0:T(8,128)S(1)}, f32[8,20]{1,0:T(8,128)S(1)}, u32[]{:S(2)}, u32[]{:S(2)}) %collective-permute-start.3) | collective-permute-done | bytes 672 | tf_op jit(solution)/shard_map/ppermute | solution.py:120
  24.1 3.1 %collective-permute-start.4 = (bf16[2,2,16,2048]{3,2,1,0:T(8,128)(2,1)S(1)}, bf16[2,2,16,2048]{3,2,1,0:T(8,128)(2,1)S(1)}, u32[]{:S(2)}, u32[]{:S(2)}) collective-permute-start(bf16[2,2,16,2048]{3,2,1,0:T(8,128)(2,1)S(1)} %pad_maximum_fusion), channel_id=1, source_target_pairs={{0,32},{32,64},{64,96},{96,0},{1,33},{33,65},{65,97},{97,1},{2,34}... | collective-permute-start | bytes 786440 | tf_op jit(solution)/shard_map/ppermute | solution.py:128
  27.2 0.0 collective-permute-start.5
  27.2 0.5 collective-permute-start.9
  27.7 4.8 %collective-permute-done.4 = bf16[2,2,16,2048]{3,2,1,0:T(8,128)(2,1)S(1)} collective-permute-done((bf16[2,2,16,2048]{3,2,1,0:T(8,128)(2,1)S(1)}, bf16[2,2,16,2048]{3,2,1,0:T(8,128)(2,1)S(1)}, u32[]{:S(2)}, u32[]{:S(2)}) %collective-permute-start.4) | collective-permute-done | bytes 262176 | tf_op jit(solution)/shard_map/ppermute | solution.py:128
  32.5 0.0 copy-start
  32.5 4.7 %collective-permute-start.6 = (bf16[1,2,16,2048]{3,2,1,0:T(8,128)(2,1)S(1)}, bf16[1,2,16,2048]{3,2,1,0:T(8,128)(2,1)S(1)}, u32[]{:S(2)}, u32[]{:S(2)}) collective-permute-start(bf16[1,2,16,2048]{3,2,1,0:T(8,128)(2,1)S(1)} %slice.90), channel_id=1, source_target_pairs={{0,32},{32,64},{64,96},{96,0},{1,33},{33,65},{65,97},{97,1},{2,34}... | collective-permute-start | bytes 393224 | tf_op jit(solution)/shard_map/ppermute | solution.py:130
  37.2 0.4 collective-permute-done.5
  37.6 1.1 %collective-permute-start.7 = (bf16[1,2,16,2048]{3,2,1,0:T(8,128)(2,1)S(1)}, bf16[1,2,16,2048]{3,2,1,0:T(8,128)(2,1)S(1)}, u32[]{:S(2)}, u32[]{:S(2)}) collective-permute-start(bf16[1,2,16,2048]{3,2,1,0:T(8,128)(2,1)S(1)} %slice.91), channel_id=1, source_target_pairs={{0,96},{32,0},{64,32},{96,64},{1,97},{33,1},{65,33},{97,65},{2,98}... | collective-permute-start | bytes 393224 | tf_op jit(solution)/shard_map/ppermute | solution.py:131
  38.7 2.9 %collective-permute-done.6 = bf16[1,2,16,2048]{3,2,1,0:T(8,128)(2,1)S(1)} collective-permute-done((bf16[1,2,16,2048]{3,2,1,0:T(8,128)(2,1)S(1)}, bf16[1,2,16,2048]{3,2,1,0:T(8,128)(2,1)S(1)}, u32[]{:S(2)}, u32[]{:S(2)}) %collective-permute-start.6) | collective-permute-done | bytes 131104 | tf_op jit(solution)/shard_map/ppermute | solution.py:130
  41.7 1.1 %collective-permute-done.7 = bf16[1,2,16,2048]{3,2,1,0:T(8,128)(2,1)S(1)} collective-permute-done((bf16[1,2,16,2048]{3,2,1,0:T(8,128)(2,1)S(1)}, bf16[1,2,16,2048]{3,2,1,0:T(8,128)(2,1)S(1)}, u32[]{:S(2)}, u32[]{:S(2)}) %collective-permute-start.7) | collective-permute-done | bytes 131104 | tf_op jit(solution)/shard_map/ppermute | solution.py:131
  42.8 0.1 collective-permute-start.8
  42.9 0.1 fusion.16
  43.0 16.0 %collective-permute-done.9.adj_par = bf16[40,128,128]{2,1,0:T(8,128)(2,1)} collective-permute-done((bf16[40,128,128]{2,1,0:T(8,128)(2,1)}, bf16[40,128,128]{2,1,0:T(8,128)(2,1)}, u32[]{:S(2)}, u32[]{:S(2)}) %collective-permute-start.9) | collective-permute-done | bytes 1310752 | tf_op jit(solution)/shard_map/ppermute | solution.py:122
  59.0 4.4 %block_products.1 = (f32[2,3,128,128]{3,2,1,0:T(8,128)S(1)}, f32[2,3,128,128]{3,2,1,0:T(8,128)S(1)}, f32[2,3,128,128]{3,2,1,0:T(8,128)S(1)}, bf16[2,3,128,128]{3...) custom-call(f32[8,20]{1,0:T(8,128)S(1)} %maximum_maximum_fusion.own,, ...), custom_call_target="tpu_custom_call" | custom-call | flops 335544320 | bytes 9437184 | tf_op jit(solution)/shard_map/block_products/pallas_call | solution.py:95
  63.4 8.5 %collective-permute-start.11 = (bf16[2,3,128,128]{3,2,1,0:T(8,128)(2,1)S(1)}, bf16[2,3,128,128]{3,2,1,0:T(8,128)(2,1)S(1)}, u32[]{:S(2)}, u32[]{:S(2)}) collective-permute-start(bf16[2,3,128,128]{3,2,1,0:T(8,128)(2,1)S(1)} %get-tuple-element.22), channel_id=1, source_target_pairs={{0,14},{2,0},{4,2},{6,4},{8,6},{10,8},{12,10},{14,12},{1,15},{3,1}... | collective-permute-start | bytes 589832 | tf_op jit(solution)/shard_map/ppermute | solution.py:146
  71.9 0.1 collective-permute-start.12
  72.0 1.5 %collective-permute-start.13 = (bf16[3,128,128]{2,1,0:T(8,128)(2,1)S(1)}, bf16[3,128,128]{2,1,0:T(8,128)(2,1)S(1)}, u32[]{:S(2)}, u32[]{:S(2)}) collective-permute-start(bf16[3,128,128]{2,1,0:T(8,128)(2,1)S(1)} %get-tuple-element.25), channel_id=1, source_target_pairs={{0,4},{2,6},{4,8},{6,10},{8,12},{10,14},{12,0},{14,2},{1,5},{3,7},... | collective-permute-start | bytes 294920 | tf_op jit(solution)/shard_map/ppermute | solution.py:146
  73.5 1.9 %collective-permute-start.15 = (bf16[2,3,128,128]{3,2,1,0:T(8,128)(2,1)S(1)}, bf16[2,3,128,128]{3,2,1,0:T(8,128)(2,1)S(1)}, u32[]{:S(2)}, u32[]{:S(2)}) collective-permute-start(bf16[2,3,128,128]{3,2,1,0:T(8,128)(2,1)S(1)} %get-tuple-element.27), channel_id=1, source_target_pairs={{0,14},{2,0},{4,2},{6,4},{8,6},{10,8},{12,10},{14,12},{1,15},{3,1}... | collective-permute-start | bytes 589832 | tf_op jit(solution)/shard_map/ppermute | solution.py:146
  75.4 1.5 %collective-permute-done.11 = bf16[2,3,128,128]{3,2,1,0:T(8,128)(2,1)S(1)} collective-permute-done((bf16[2,3,128,128]{3,2,1,0:T(8,128)(2,1)S(1)}, bf16[2,3,128,128]{3,2,1,0:T(8,128)(2,1)S(1)}, u32[]{:S(2)}, u32[]{:S(2)}) %collective-permute-start.11) | collective-permute-done | bytes 196640 | tf_op jit(solution)/shard_map/ppermute | solution.py:146
  76.9 1.4 %collective-permute-start.19 = (bf16[3,128,128]{2,1,0:T(8,128)(2,1)S(1)}, bf16[3,128,128]{2,1,0:T(8,128)(2,1)S(1)}, u32[]{:S(2)}, u32[]{:S(2)}) collective-permute-start(bf16[3,128,128]{2,1,0:T(8,128)(2,1)S(1)} %get-tuple-element.28), channel_id=1, source_target_pairs={{0,12},{2,14},{4,0},{6,2},{8,4},{10,6},{12,8},{14,10},{1,13},{3,15... | collective-permute-start | bytes 294920 | tf_op jit(solution)/shard_map/ppermute | solution.py:146
  78.3 2.6 %collective-permute-done.10 = bf16[2,3,128,128]{3,2,1,0:T(8,128)(2,1)S(1)} collective-permute-done((bf16[2,3,128,128]{3,2,1,0:T(8,128)(2,1)S(1)}, bf16[2,3,128,128]{3,2,1,0:T(8,128)(2,1)S(1)}, u32[]{:S(2)}, u32[]{:S(2)}) %collective-permute-start.10) | collective-permute-done | bytes 196640 | tf_op jit(solution)/shard_map/ppermute | solution.py:146
  81.0 0.6 collective-permute-start.17
  81.6 5.1 %collective-permute-done.12 = bf16[2,3,128,128]{3,2,1,0:T(8,128)(2,1)S(1)} collective-permute-done((bf16[2,3,128,128]{3,2,1,0:T(8,128)(2,1)S(1)}, bf16[2,3,128,128]{3,2,1,0:T(8,128)(2,1)S(1)}, u32[]{:S(2)}, u32[]{:S(2)}) %collective-permute-start.12) | collective-permute-done | bytes 196640 | tf_op jit(solution)/shard_map/ppermute | solution.py:146
  86.8 0.1 collective-permute-start.18
  87.0 6.6 %collective-permute-start.20 = (bf16[3,128,128]{2,1,0:T(8,128)(2,1)S(1)}, bf16[3,128,128]{2,1,0:T(8,128)(2,1)S(1)}, u32[]{:S(2)}, u32[]{:S(2)}) collective-permute-start(bf16[3,128,128]{2,1,0:T(8,128)(2,1)S(1)} %fusion.5), channel_id=1, source_target_pairs={{0,13},{1,12},{2,15},{3,14},{4,1},{5,0},{6,3},{7,2},{8,5},{9,4},{1... | collective-permute-start | bytes 294920 | tf_op jit(solution)/shard_map/ppermute | solution.py:149
  93.6 0.0 copy-start.2
  93.6 0.1 collective-permute-start.14
  93.7 4.1 %collective-permute-start.16 = (bf16[3,128,128]{2,1,0:T(8,128)(2,1)S(1)}, bf16[3,128,128]{2,1,0:T(8,128)(2,1)S(1)}, u32[]{:S(2)}, u32[]{:S(2)}) collective-permute-start(bf16[3,128,128]{2,1,0:T(8,128)(2,1)S(1)} %fusion.17), channel_id=1, source_target_pairs={{0,12},{2,14},{4,0},{6,2},{8,4},{10,6},{12,8},{14,10},{1,13},{3,15... | collective-permute-start | bytes 294920 | tf_op jit(solution)/shard_map/ppermute | solution.py:146
  97.9 0.2 collective-permute-done.18
  98.1 0.2 fusion.20
  98.3 2.2 %collective-permute-done.14 = bf16[3,128,128]{2,1,0:T(8,128)(2,1)S(1)} collective-permute-done((bf16[3,128,128]{2,1,0:T(8,128)(2,1)S(1)}, bf16[3,128,128]{2,1,0:T(8,128)(2,1)S(1)}, u32[]{:S(2)}, u32[]{:S(2)}) %collective-permute-start.14) | collective-permute-done | bytes 98336 | tf_op jit(solution)/shard_map/ppermute | solution.py:146
  100.4 0.1 fusion.15
  100.5 0.9 fusion.2
  (33 shorter events, 0.5 us)
Async XLA Ops:
  0.0 5.4 %collective-permute-start = (bf16[2,16,2048]{2,1,0:T(8,128)(2,1)}, bf16[2,16,2048]{2,1,0:T(8,128)(2,1)S(1)}, u32[]{:S(2)}, u32[]{:S(2)}) collective-permute-start(bf16[2,16,2048]{2,1,0:T(8,128)(2,1)} %param.13), channel_id=1, source_target_pairs={{0,128},{128,0},{1,129},{129,1},{2,130},{130,2},{3,131},{131,3},{4... | collective-permute-start | bytes 393224 | tf_op jit(solution)/shard_map/ppermute | solution.py:110
  6.4 14.2 %collective-permute-start.1 = (bf16[2,16,2048]{2,1,0:T(8,128)(2,1)S(1)}, bf16[2,16,2048]{2,1,0:T(8,128)(2,1)S(1)}, u32[]{:S(2)}, u32[]{:S(2)}) collective-permute-start(bf16[2,16,2048]{2,1,0:T(8,128)(2,1)S(1)} %get-tuple-element.29), channel_id=1, source_target_pairs={{0,0},{2,32},{4,64},{6,96},{8,8},{10,40},{12,72},{14,104},{32,2},{... | collective-permute-start | bytes 393224 | tf_op jit(solution)/shard_map/ppermute | solution.py:125
  10.1 12.6 %collective-permute-start.2 = (bf16[2,16,2048]{2,1,0:T(8,128)(2,1)S(1)}, bf16[2,16,2048]{2,1,0:T(8,128)(2,1)S(1)}, u32[]{:S(2)}, u32[]{:S(2)}) collective-permute-start(bf16[2,16,2048]{2,1,0:T(8,128)(2,1)S(1)} %get-tuple-element.30), channel_id=1, source_target_pairs={{0,8},{2,40},{4,72},{6,104},{8,0},{10,32},{12,64},{14,96},{32,10},... | collective-permute-start | bytes 393224 | tf_op jit(solution)/shard_map/ppermute | solution.py:126
  18.9 5.1 %collective-permute-start.3 = (f32[8,20]{1,0:T(8,128)S(1)}, f32[8,20]{1,0:T(8,128)S(1)}, u32[]{:S(2)}, u32[]{:S(2)}) collective-permute-start(f32[8,20]{1,0:T(8,128)S(1)} %maximum_maximum_fusion.own), channel_id=1, source_target_pairs={{0,1},{1,0},{2,3},{3,2},{4,5},{5,4},{6,7},{7,6},{8,9},{9,8},{10,11... | collective-permute-start | bytes 1928 | tf_op jit(solution)/shard_map/ppermute | solution.py:120
  24.1 8.4 %collective-permute-start.4 = (bf16[2,2,16,2048]{3,2,1,0:T(8,128)(2,1)S(1)}, bf16[2,2,16,2048]{3,2,1,0:T(8,128)(2,1)S(1)}, u32[]{:S(2)}, u32[]{:S(2)}) collective-permute-start(bf16[2,2,16,2048]{3,2,1,0:T(8,128)(2,1)S(1)} %pad_maximum_fusion), channel_id=1, source_target_pairs={{0,32},{32,64},{64,96},{96,0},{1,33},{33,65},{65,97},{97,1},{2,34}... | collective-permute-start | bytes 786440 | tf_op jit(solution)/shard_map/ppermute | solution.py:128
  27.2 10.4 %collective-permute-start.5 = (bf16[2,2,16,2048]{3,2,1,0:T(8,128)(2,1)S(1)}, bf16[2,2,16,2048]{3,2,1,0:T(8,128)(2,1)S(1)}, u32[]{:S(2)}, u32[]{:S(2)}) collective-permute-start(bf16[2,2,16,2048]{3,2,1,0:T(8,128)(2,1)S(1)} %pad_maximum_fusion), channel_id=1, source_target_pairs={{0,96},{32,0},{64,32},{96,64},{1,97},{33,1},{65,33},{97,65},{2,98}... | collective-permute-start | bytes 786440 | tf_op jit(solution)/shard_map/ppermute | solution.py:129
  27.2 15.7 %copy-start.1 = (bf16[256,256]{1,0:T(8,128)(2,1)S(1)}, bf16[256,256]{1,0:T(8,128)(2,1)}, u32[]{:S(2)}) copy-start(bf16[256,256]{1,0:T(8,128)(2,1)} %param.14) | copy-start | bytes 393220
  27.2 31.8 %collective-permute-start.9 = (bf16[40,128,128]{2,1,0:T(8,128)(2,1)}, bf16[40,128,128]{2,1,0:T(8,128)(2,1)}, u32[]{:S(2)}, u32[]{:S(2)}) collective-permute-start(bf16[40,128,128]{2,1,0:T(8,128)(2,1)} %bitcast.59), channel_id=1, source_target_pairs={{0,1},{1,0},{2,3},{3,2},{4,5},{5,4},{6,7},{7,6},{8,9},{9,8},{10,11... | collective-permute-start | bytes 3932168 | tf_op jit(solution)/shard_map/ppermute | solution.py:122
  32.5 26.5 %copy-start = (bf16[2,1,1,20,128,128]{5,4,3,2,1,0:T(8,128)(2,1)S(1)}, bf16[2,1,1,20,128,128]{5,4,3,2,1,0:T(8,128)(2,1)}, u32[]{:S(2)}) copy-start(bf16[2,1,1,20,128,128]{5,4,3,2,1,0:T(8,128)(2,1)} %param.8) | copy-start | bytes 3932164
  32.5 9.1 %collective-permute-start.6 = (bf16[1,2,16,2048]{3,2,1,0:T(8,128)(2,1)S(1)}, bf16[1,2,16,2048]{3,2,1,0:T(8,128)(2,1)S(1)}, u32[]{:S(2)}, u32[]{:S(2)}) collective-permute-start(bf16[1,2,16,2048]{3,2,1,0:T(8,128)(2,1)S(1)} %slice.90), channel_id=1, source_target_pairs={{0,32},{32,64},{64,96},{96,0},{1,33},{33,65},{65,97},{97,1},{2,34}... | collective-permute-start | bytes 393224 | tf_op jit(solution)/shard_map/ppermute | solution.py:130
  37.6 5.2 %collective-permute-start.7 = (bf16[1,2,16,2048]{3,2,1,0:T(8,128)(2,1)S(1)}, bf16[1,2,16,2048]{3,2,1,0:T(8,128)(2,1)S(1)}, u32[]{:S(2)}, u32[]{:S(2)}) collective-permute-start(bf16[1,2,16,2048]{3,2,1,0:T(8,128)(2,1)S(1)} %slice.91), channel_id=1, source_target_pairs={{0,96},{32,0},{64,32},{96,64},{1,97},{33,1},{65,33},{97,65},{2,98}... | collective-permute-start | bytes 393224 | tf_op jit(solution)/shard_map/ppermute | solution.py:131
  42.8 16.3 %collective-permute-start.8 = (bf16[8,2,16,2048]{3,2,1,0:T(8,128)(2,1)S(1)}, bf16[8,2,16,2048]{3,2,1,0:T(8,128)(2,1)S(1)}, u32[]{:S(2)}, u32[]{:S(2)}) collective-permute-start(bf16[8,2,16,2048]{3,2,1,0:T(8,128)(2,1)S(1)} %constant_dynamic-update-slice_fusion.feats0), channel_id=1, source_target_pairs={{0,16},{16,0},{1,17},{17,1},{2,18},{18,2},{3,19},{19,3},{4,20},{20... | collective-permute-start | bytes 3145736 | tf_op jit(solution)/shard_map/ppermute | solution.py:133
  63.4 13.5 %collective-permute-start.11 = (bf16[2,3,128,128]{3,2,1,0:T(8,128)(2,1)S(1)}, bf16[2,3,128,128]{3,2,1,0:T(8,128)(2,1)S(1)}, u32[]{:S(2)}, u32[]{:S(2)}) collective-permute-start(bf16[2,3,128,128]{3,2,1,0:T(8,128)(2,1)S(1)} %get-tuple-element.22), channel_id=1, source_target_pairs={{0,14},{2,0},{4,2},{6,4},{8,6},{10,8},{12,10},{14,12},{1,15},{3,1}... | collective-permute-start | bytes 589832 | tf_op jit(solution)/shard_map/ppermute | solution.py:146
  71.9 9.0 %collective-permute-start.10 = (bf16[2,3,128,128]{3,2,1,0:T(8,128)(2,1)S(1)}, bf16[2,3,128,128]{3,2,1,0:T(8,128)(2,1)S(1)}, u32[]{:S(2)}, u32[]{:S(2)}) collective-permute-start(bf16[2,3,128,128]{3,2,1,0:T(8,128)(2,1)S(1)} %get-tuple-element.21), channel_id=1, source_target_pairs={{0,2},{2,4},{4,6},{6,8},{8,10},{10,12},{12,14},{14,0},{1,3},{3,5},... | collective-permute-start | bytes 589832 | tf_op jit(solution)/shard_map/ppermute | solution.py:146
  71.9 14.8 %collective-permute-start.12 = (bf16[2,3,128,128]{3,2,1,0:T(8,128)(2,1)S(1)}, bf16[2,3,128,128]{3,2,1,0:T(8,128)(2,1)S(1)}, u32[]{:S(2)}, u32[]{:S(2)}) collective-permute-start(bf16[2,3,128,128]{3,2,1,0:T(8,128)(2,1)S(1)} %get-tuple-element.24), channel_id=1, source_target_pairs={{0,2},{2,4},{4,6},{6,8},{8,10},{10,12},{12,14},{14,0},{1,3},{3,5},... | collective-permute-start | bytes 589832 | tf_op jit(solution)/shard_map/ppermute | solution.py:146
  72.0 21.5 %collective-permute-start.13 = (bf16[3,128,128]{2,1,0:T(8,128)(2,1)S(1)}, bf16[3,128,128]{2,1,0:T(8,128)(2,1)S(1)}, u32[]{:S(2)}, u32[]{:S(2)}) collective-permute-start(bf16[3,128,128]{2,1,0:T(8,128)(2,1)S(1)} %get-tuple-element.25), channel_id=1, source_target_pairs={{0,4},{2,6},{4,8},{6,10},{8,12},{10,14},{12,0},{14,2},{1,5},{3,7},... | collective-permute-start | bytes 294920 | tf_op jit(solution)/shard_map/ppermute | solution.py:146
  73.5 13.4 %collective-permute-start.15 = (bf16[2,3,128,128]{3,2,1,0:T(8,128)(2,1)S(1)}, bf16[2,3,128,128]{3,2,1,0:T(8,128)(2,1)S(1)}, u32[]{:S(2)}, u32[]{:S(2)}) collective-permute-start(bf16[2,3,128,128]{3,2,1,0:T(8,128)(2,1)S(1)} %get-tuple-element.27), channel_id=1, source_target_pairs={{0,14},{2,0},{4,2},{6,4},{8,6},{10,8},{12,10},{14,12},{1,15},{3,1}... | collective-permute-start | bytes 589832 | tf_op jit(solution)/shard_map/ppermute | solution.py:146
  76.9 10.0 %collective-permute-start.19 = (bf16[3,128,128]{2,1,0:T(8,128)(2,1)S(1)}, bf16[3,128,128]{2,1,0:T(8,128)(2,1)S(1)}, u32[]{:S(2)}, u32[]{:S(2)}) collective-permute-start(bf16[3,128,128]{2,1,0:T(8,128)(2,1)S(1)} %get-tuple-element.28), channel_id=1, source_target_pairs={{0,12},{2,14},{4,0},{6,2},{8,4},{10,6},{12,8},{14,10},{1,13},{3,15... | collective-permute-start | bytes 294920 | tf_op jit(solution)/shard_map/ppermute | solution.py:146
  81.0 16.9 %collective-permute-start.17 = (bf16[3,128,128]{2,1,0:T(8,128)(2,1)S(1)}, bf16[3,128,128]{2,1,0:T(8,128)(2,1)S(1)}, u32[]{:S(2)}, u32[]{:S(2)}) collective-permute-start(bf16[3,128,128]{2,1,0:T(8,128)(2,1)S(1)} %fusion.18), channel_id=1, source_target_pairs={{0,1},{1,0},{2,3},{3,2},{4,5},{5,4},{6,7},{7,6},{8,9},{9,8},{10,11... | collective-permute-start | bytes 294920 | tf_op jit(solution)/shard_map/ppermute | solution.py:158
  86.8 11.2 %collective-permute-start.18 = (bf16[3,128,128]{2,1,0:T(8,128)(2,1)S(1)}, bf16[3,128,128]{2,1,0:T(8,128)(2,1)S(1)}, u32[]{:S(2)}, u32[]{:S(2)}) collective-permute-start(bf16[3,128,128]{2,1,0:T(8,128)(2,1)S(1)} %fusion.19), channel_id=1, source_target_pairs={{0,5},{1,4},{2,7},{3,6},{4,9},{5,8},{6,11},{7,10},{8,13},{9,12},{1... | collective-permute-start | bytes 294920 | tf_op jit(solution)/shard_map/ppermute | solution.py:149
  87.0 11.1 %collective-permute-start.20 = (bf16[3,128,128]{2,1,0:T(8,128)(2,1)S(1)}, bf16[3,128,128]{2,1,0:T(8,128)(2,1)S(1)}, u32[]{:S(2)}, u32[]{:S(2)}) collective-permute-start(bf16[3,128,128]{2,1,0:T(8,128)(2,1)S(1)} %fusion.5), channel_id=1, source_target_pairs={{0,13},{1,12},{2,15},{3,14},{4,1},{5,0},{6,3},{7,2},{8,5},{9,4},{1... | collective-permute-start | bytes 294920 | tf_op jit(solution)/shard_map/ppermute | solution.py:149
  93.6 6.9 %copy-start.2 = (f32[256]{0:T(256)S(1)}, f32[256]{0:T(256)}, u32[]{:S(2)}) copy-start(f32[256]{0:T(256)} %param.15) | copy-start | bytes 3076
  93.6 6.8 %collective-permute-start.14 = (bf16[3,128,128]{2,1,0:T(8,128)(2,1)S(1)}, bf16[3,128,128]{2,1,0:T(8,128)(2,1)S(1)}, u32[]{:S(2)}, u32[]{:S(2)}) collective-permute-start(bf16[3,128,128]{2,1,0:T(8,128)(2,1)S(1)} %fusion.11), channel_id=1, source_target_pairs={{0,4},{2,6},{4,8},{6,10},{8,12},{10,14},{12,0},{14,2},{1,5},{3,7},... | collective-permute-start | bytes 294920 | tf_op jit(solution)/shard_map/ppermute | solution.py:146
  93.7 6.7 %collective-permute-start.16 = (bf16[3,128,128]{2,1,0:T(8,128)(2,1)S(1)}, bf16[3,128,128]{2,1,0:T(8,128)(2,1)S(1)}, u32[]{:S(2)}, u32[]{:S(2)}) collective-permute-start(bf16[3,128,128]{2,1,0:T(8,128)(2,1)S(1)} %fusion.17), channel_id=1, source_target_pairs={{0,12},{2,14},{4,0},{6,2},{8,4},{10,6},{12,8},{14,10},{1,13},{3,15... | collective-permute-start | bytes 294920 | tf_op jit(solution)/shard_map/ppermute | solution.py:146
